TPU v7x, 256 devices: a whole 4x4x8 slice. The times are simulated.
256 devices in a mesh: row: 8 (over z), col: 16 (over x_hi, y, core), pan: 2 (over x_lo).
Axes of the slice: x: 4 (x_hi: 2, x_lo: 2; x = x_hi * 2 + x_lo), y: 4, z: 8, core: 2. Of those that a mesh axis runs over, the one named last changes fastest.
Arguments:
- gradient: bfloat16 [8192, 28672], P('row', ('col', 'pan')), may hold values from -240 to 240
- stat_old: float32 [8192, 1024], P(('row', 'col', 'pan')), may hold values from -4800 to 4800, as said below
Outputs:
- preconditioned: float32 [8192, 28672], P('row', ('col', 'pan'))
- stat_new: float32 [8192, 1024], P(('row', 'col', 'pan'))
Inputs may be any that keep to these rules, and one draw needn't show every extreme that they name: Each block of 1024 rows of stat_old is a symmetric positive definite matrix.
All inputs are finite; a program needn't handle non-finite values.
Results may differ from a plain program's by a relative error of at most 0.0003.
Values sent between devices are 32-bit elements; how exact they have to be, the bound alone decides.
No kernel may reach another device: no remote copies, remote signals or barrier semaphores. Data moves between devices by JAX's collectives and lax.ppermute only.
A program may use at most 64 MiB of HBM per device.

v0:
```python
import jax
import jax.numpy as jnp
from jax import lax
from jax.sharding import PartitionSpec as P

COLS = 28672
damping = 0.001
stat_decay = 0.9
newton_scale = 2.5


def local(gradient, stat_old):
    highest = lax.Precision.HIGHEST
    panel_rows = stat_old.shape[0]
    order_size = stat_old.shape[1]
    offset = lax.axis_index(("col", "pan")) * panel_rows
    weight_new = (1.0 - stat_decay) / COLS
    row_ids = lax.broadcasted_iota(jnp.int32, (panel_rows, order_size), 0) + offset
    col_ids = lax.broadcasted_iota(jnp.int32, (panel_rows, order_size), 1)
    eye_panel = (row_ids == col_ids).astype(jnp.float32)
    eye_whole = jnp.eye(order_size, dtype=jnp.float32)
    contract = (((1,), (1,)), ((), ()))
    partial_value = lax.dot_general(
        gradient, gradient, contract, preferred_element_type=jnp.float32
    )
    placed = lax.dynamic_update_slice_in_dim(
        jnp.zeros((order_size, order_size), jnp.float32), stat_decay * stat_old, offset, 0
    )
    stat_whole = lax.psum(weight_new * partial_value + placed, ("col", "pan"))
    stat_new = lax.dynamic_slice_in_dim(stat_whole, offset, panel_rows, 0)
    matrix = stat_whole + damping * eye_whole
    frobenius = jnp.sqrt(jnp.sum(matrix * matrix))
    scaled = newton_scale * matrix / frobenius
    first_step = 1.25 * eye_whole - 0.25 * scaled
    square = jnp.dot(first_step, first_step, precision=highest)
    square_panel = lax.dynamic_slice_in_dim(square, offset, panel_rows, 0)
    fourth_panel = jnp.dot(square_panel, square, precision=highest)
    moved_panel = jnp.dot(fourth_panel, scaled, precision=highest)
    second_panel = 1.25 * eye_panel - 0.25 * moved_panel
    product = jnp.dot(second_panel, first_step, precision=highest)
    root_panel = (frobenius / newton_scale) ** (-0.25) * product
    preconditioned = jnp.dot(
        lax.all_gather(root_panel, ("col", "pan"), axis=0, tiled=True),
        gradient,
        precision=highest,
        preferred_element_type=jnp.float32,
    )
    return (preconditioned, stat_new)


def solution(mesh):
    placed = (P("row", ("col", "pan")), P(("row", "col", "pan"), None))
    return jax.shard_map(
        local,
        mesh=mesh,
        in_specs=placed,
        out_specs=(P("row", ("col", "pan")), P(("row", "col", "pan"), None)),
        check_vma=False,
    )
```

profile of v0, /device:TPU:1, one launch (start us, length us, event | category | flops | bytes accessed | tf_op | source)
XLA Modules:
  0.0 281.0 jit_solution(15637310542160839473)
XLA Ops:
  7.2 0.0 copy-start
  7.2 0.0 all-reduce.2.cloned.1.call-start
  7.2 1.4 copy-done
  8.7 0.0 copy-start.2
  8.7 4.3 %convolution_multiply_fusion = f32[1024,1024]{1,0:T(8,128)} fusion(bf16[1024,896]{1,0:T(8,128)(2,1)S(1)} %copy-done), kind=kOutput, calls=%fused_computation.7 | convolution fusion | flops 1880096768 | bytes 6029312 | tf_op jit(solution)/shard_map/dot_general | solution.py:23
  13.0 0.0 copy-done.2
  13.0 1.6 add_dynamic-update-slice_fusion
  14.6 0.0 all-reduce.2.cloned.1.call-update
  14.6 0.0 all-gather.2.cloned.1.call-start
  14.7 125.5 %all-reduce.2.cloned.1.call-done = f32[1024,1024]{1,0:T(8,128)} async-done(((f32[1024,1024]{1,0:T(8,128)}), f32[1024,1024]{1,0:T(8,128)}) %all-reduce.2.cloned.1.call-update) | async-done | bytes 4194320 | tf_op jit(solution)/shard_map/psum | solution.py:29
  140.2 3.9 %multiply_reduce_fusion = f32[]{:T(128)} fusion(f32[1024,1024]{1,0:T(8,128)} %all-reduce.2.cloned.1.call-done), kind=kLoop, calls=%fused_computation.2 | loop fusion | flops 5242879 | bytes 4194308 | tf_op jit(solution)/shard_map/reduce_sum | solution.py:32
  144.8 19.9 %fusion.1 = f32[1024,1024]{1,0:T(8,128)S(1)} fusion(f32[1024,1024]{1,0:T(8,128)} %all-reduce.2.cloned.1.call-done, f32[]{:T(128)S(6)} %sqrt.3), kind=kOutput, calls=%fused_computation.6 | convolution fusion | flops 12893290496 | bytes 8388612 | tf_op jit(solution)/shard_map/dot_general | solution.py:35
  164.7 2.5 fusion.10
  167.2 0.0 copy-start.1
  167.2 5.1 %fusion.8 = f32[32,1024]{1,0:T(8,128)S(1)} fusion(f32[32,1024]{1,0:T(8,128)S(1)} %fusion.10, s32[32]{0:T(128)S(1)} %iota_add_fusion, f32[1024,1024]{1,0:T(8,128)} %all-reduce.2.cloned.1.call-done, f32[]{:T(128)S(6)} %sqrt.3), kind=kOutput, calls=%fused_computation.15 | convolution fusion | flops 408027136 | bytes 4456580 | tf_op jit(solution)/shard_map/dot_general | solution.py:38
  172.4 0.0 copy-done.1
  172.4 3.7 %fusion.9 = f32[32,1024]{1,0:T(8,128)} fusion(f32[32,1024]{1,0:T(8,128)S(1)} %fusion.8, f32[]{:T(128)S(6)} %pow.3, f32[1024,1024]{1,0:T(8,128)S(1)} %copy-done.1, f32[]{:T(128)S(6)} %sqrt.3), kind=kOutput, calls=%fused_computation.16 | convolution fusion | flops 411074560 | bytes 4456456 | tf_op jit(solution)/shard_map/dot_general | solution.py:40
  176.1 0.0 all-gather.2.cloned.1.call-update
  176.1 1.6 constant_dynamic-slice_fusion
  177.7 86.8 %all-gather.2.cloned.1.call-done = f32[1024,1024]{1,0:T(8,128)} async-done(((f32[32,1024]{1,0:T(8,128)}), f32[1024,1024]{1,0:T(8,128)}) %all-gather.2.cloned.1.call-update) | async-done | bytes 4194320 | tf_op jit(solution)/shard_map/all_gather | solution.py:43
  264.5 9.6 %fusion.19 = f32[1024,896]{1,0:T(8,128)} fusion(f32[1024,1024]{1,0:T(8,128)} %all-gather.2.cloned.1.call-done, bf16[1024,896]{1,0:T(8,128)(2,1)S(1)} %copy-done), kind=kOutput, calls=%fused_computation.30 | convolution fusion | flops 11274289152 | bytes 9699328 | tf_op jit(solution)/shard_map/dot_general | solution.py:42
  (1 shorter events, 0.0 us)
Async XLA Ops:
  7.2 1.5 copy-start
  7.2 133.0 %all-reduce.2.cloned.1.call-start = ((), (), s32[]{:S(2)}) async-start(), calls=%async_computation | async-start | bytes 8388608 | tf_op jit(solution)/shard_map/psum | solution.py:29
  8.7 4.3 %copy-start.2 = (f32[32,1024]{1,0:T(8,128)S(1)}, f32[32,1024]{1,0:T(8,128)}, u32[]{:S(2)}) copy-start(f32[32,1024]{1,0:T(8,128)} %param.3) | copy-start | bytes 393220
  14.6 249.9 %all-gather.2.cloned.1.call-start = ((), (), s32[]{:S(2)}) async-start(), calls=%async_computation.1 | async-start | bytes 4325376 | tf_op jit(solution)/shard_map/all_gather | solution.py:43
  167.2 5.1 %copy-start.1 = (f32[1024,1024]{1,0:T(8,128)S(1)}, f32[1024,1024]{1,0:T(8,128)}, u32[]{:S(2)}) copy-start(f32[1024,1024]{1,0:T(8,128)} %all-reduce.2.cloned.1.call-done) | copy-start | bytes 12582916
Sparse Core Ops, SparseCore 0:
  14.7 125.4 all-reduce.1
  176.3 88.1 all-gather.1
where the time goes:
time: 281 us
  waiting for transfers between devices  212 us (75%)
  matrix products  45.2 us (16%)
  between operations  14.9 us (5%)
  other arithmetic  5.45 us (2%)
  local copies, waits for them, and re-layouts  3.03 us (1%)
    psum x1, waiting for transfers between devices, local(): stat_whole = lax.psum(weight_new * partial_value + placed, ('col', 'pan'))  126 us
    all_gather x1, waiting for transfers between devices, local(): lax.all_gather(root_panel, ('col', 'pan'), axis=0, tiled=True)  86.8 us
    dot_general x1, matrix products, local(): square = jnp.dot(first_step, first_step, precision=highest)  19.9 us
    dot_general x1, matrix products, local(): jnp.dot(lax.all_gather(root_panel, ('col', 'pan'), axis=0, tiled=True), g...  9.65 us
  transfers between devices with their start and end apart: 2, of which 2 were waited for; matrix products, arithmetic and copies ran while one was open for 1% of the time, Pallas kernels for 0%

commit v1 on v0

--- a/solution.py
+++ b/solution.py
@@ -40,7 +40,12 @@
     product = jnp.dot(second_panel, first_step, precision=highest)
     root_panel = (frobenius / newton_scale) ** (-0.25) * product
     preconditioned = jnp.dot(
-        lax.all_gather(root_panel, ("col", "pan"), axis=0, tiled=True),
+        jnp.concatenate(
+            lax.all_to_all(
+                jnp.stack([root_panel] * lax.axis_size(("col", "pan"))), ("col", "pan"), 0, 0
+            ),
+            axis=0,
+        ),
         gradient,
         precision=highest,
         preferred_element_type=jnp.float32,

time: 281 us -> 255 us (0.907); the launches traced: 281 us -> 251 us
  waiting for transfers between devices: 212 us -> 175 us
  starting transfers between devices: 0.08 us -> 5.99 us
    all_gather x1 -> x0, waiting for transfers between devices: 86.8 us -> none  [local(): lax.all_gather(root_panel, ('col', 'pan'), axis=0, tiled=True)]
    all_to_all x0 -> x1, waiting for transfers between devices: none -> 49.3 us  [local(): lax.all_to_all(jnp.stack([root_panel] * lax.axis_size(('col', 'pan'))), (...]
    all_to_all x0 -> x1, starting transfers between devices: none -> 5.95 us  [local(): lax.all_to_all(jnp.stack([root_panel] * lax.axis_size(('col', 'pan'))), (...]
where the time goes in v1:
time: 255 us; the launch traced here: 251 us
  waiting for transfers between devices  175 us (69%)
  matrix products  44.6 us (17%)
  between operations  14.9 us (6%)
  starting transfers between devices  5.99 us (2%)
  local copies, waits for them, and re-layouts  5.51 us (2%)
  other arithmetic  5.46 us (2%)
    psum x1, waiting for transfers between devices, local(): stat_whole = lax.psum(weight_new * partial_value + placed, ('col', 'pan'))  126 us
    all_to_all x1, waiting for transfers between devices, local(): lax.all_to_all(jnp.stack([root_panel] * lax.axis_size(('col', 'pan'))), (...  49.3 us
    dot_general x1, matrix products, local(): square = jnp.dot(first_step, first_step, precision=highest)  19.9 us
    dot_general x1, matrix products, local(): jnp.dot(jnp.concatenate(lax.all_to_all(jnp.stack([root_panel] * lax.axis_...  9.65 us
    all_to_all x1, starting transfers between devices, local(): lax.all_to_all(jnp.stack([root_panel] * lax.axis_size(('col', 'pan'))), (...  5.95 us
    dot_general x1, matrix products, local(): moved_panel = jnp.dot(fourth_panel, scaled, precision=highest)  5.12 us
  transfers between devices with their start and end apart: 2, of which 2 were waited for; matrix products, arithmetic and copies ran while one was open for 1% of the time, Pallas kernels for 0%

profile of v1, /device:TPU:1, one launch (start us, length us, event | category | flops | bytes accessed | tf_op | source)
XLA Modules:
  0.0 251.3 jit_solution(7673776842577927502)
XLA Ops:
  7.2 0.0 copy-start
  7.2 0.0 all-reduce.2.cloned.1.call-start
  7.2 1.4 copy-done
  8.7 0.0 copy-start.2
  8.7 4.3 %convolution_multiply_fusion = f32[1024,1024]{1,0:T(8,128)} fusion(bf16[1024,896]{1,0:T(8,128)(2,1)S(1)} %copy-done), kind=kOutput, calls=%fused_computation.7 | convolution fusion | flops 1880096768 | bytes 6029312 | tf_op jit(solution)/shard_map/dot_general | solution.py:23
  13.0 0.0 copy-done.2
  13.0 1.6 add_dynamic-update-slice_fusion
  14.6 0.0 all-reduce.2.cloned.1.call-update
  14.6 125.7 %all-reduce.2.cloned.1.call-done = f32[1024,1024]{1,0:T(8,128)} async-done(((f32[1024,1024]{1,0:T(8,128)}), f32[1024,1024]{1,0:T(8,128)}) %all-reduce.2.cloned.1.call-update) | async-done | bytes 4194320 | tf_op jit(solution)/shard_map/psum | solution.py:29
  140.3 3.9 %multiply_reduce_fusion = f32[]{:T(128)} fusion(f32[1024,1024]{1,0:T(8,128)} %all-reduce.2.cloned.1.call-done), kind=kLoop, calls=%fused_computation.2 | loop fusion | flops 5242879 | bytes 4194308 | tf_op jit(solution)/shard_map/reduce_sum | solution.py:32
  144.9 19.9 %fusion.1 = f32[1024,1024]{1,0:T(8,128)S(1)} fusion(f32[1024,1024]{1,0:T(8,128)} %all-reduce.2.cloned.1.call-done, f32[]{:T(128)S(6)} %sqrt.3), kind=kOutput, calls=%fused_computation.6 | convolution fusion | flops 12893290496 | bytes 8388612 | tf_op jit(solution)/shard_map/dot_general | solution.py:35
  164.8 2.5 fusion.10
  167.3 0.0 copy-start.1
  167.3 5.1 %fusion.8 = f32[32,1024]{1,0:T(8,128)S(1)} fusion(f32[32,1024]{1,0:T(8,128)S(1)} %fusion.10, s32[32]{0:T(128)S(1)} %iota_add_fusion, f32[1024,1024]{1,0:T(8,128)} %all-reduce.2.cloned.1.call-done, f32[]{:T(128)S(6)} %sqrt.3), kind=kOutput, calls=%fused_computation.15 | convolution fusion | flops 408027136 | bytes 4456580 | tf_op jit(solution)/shard_map/dot_general | solution.py:38
  172.5 0.0 copy-done.1
  172.5 3.1 %fusion.9 = f32[32,1024]{1,0:T(8,128)S(1)} fusion(f32[32,1024]{1,0:T(8,128)S(1)} %fusion.8, f32[]{:T(128)S(6)} %pow.3, f32[1024,1024]{1,0:T(8,128)S(1)} %copy-done.1, f32[]{:T(128)S(6)} %sqrt.3), kind=kOutput, calls=%fused_computation.16 | convolution fusion | flops 411074560 | bytes 4456456 | tf_op jit(solution)/shard_map/dot_general | solution.py:40
  175.5 2.5 stack.2
  178.0 6.0 %all-to-all-start = ((f32[32,32,1024]{2,1,0:T(8,128)}), f32[32,32,1024]{2,1,0:T(8,128)}, u32[]{:S(2)}, u32[]{:S(2)}) async-start(f32[32,32,1024]{2,1,0:T(8,128)} %stack.2), calls=%async_computation | async-start | bytes 8388608 | tf_op jit(solution)/shard_map/all_to_all | solution.py:44
  184.0 1.6 constant_dynamic-slice_fusion
  185.6 49.3 %all-to-all-done = f32[32,32,1024]{2,1,0:T(8,128)} async-done(((f32[32,32,1024]{2,1,0:T(8,128)}), f32[32,32,1024]{2,1,0:T(8,128)}, u32[]{:S(2)}, u32[]{:S(2)}) %all-to-all-start) | async-done | bytes 4194336 | tf_op jit(solution)/shard_map/all_to_all | solution.py:44
  234.8 9.6 %fusion.19 = f32[1024,896]{1,0:T(8,128)} fusion(f32[1024,1024]{1,0:T(8,128)} %bitcast, bf16[1024,896]{1,0:T(8,128)(2,1)S(1)} %copy-done), kind=kOutput, calls=%fused_computation.30 | convolution fusion | flops 11274289152 | bytes 9699328 | tf_op jit(solution)/shard_map/dot_general | solution.py:42
  (1 shorter events, 0.0 us)
Async XLA Ops:
  7.2 1.5 copy-start
  7.2 133.1 %all-reduce.2.cloned.1.call-start = ((), (), s32[]{:S(2)}) async-start(), calls=%async_computation.1 | async-start | bytes 8388608 | tf_op jit(solution)/shard_map/psum | solution.py:29
  8.7 4.3 %copy-start.2 = (f32[32,1024]{1,0:T(8,128)S(1)}, f32[32,1024]{1,0:T(8,128)}, u32[]{:S(2)}) copy-start(f32[32,1024]{1,0:T(8,128)} %param.3) | copy-start | bytes 393220
  167.3 5.1 %copy-start.1 = (f32[1024,1024]{1,0:T(8,128)S(1)}, f32[1024,1024]{1,0:T(8,128)}, u32[]{:S(2)}) copy-start(f32[1024,1024]{1,0:T(8,128)} %all-reduce.2.cloned.1.call-done) | copy-start | bytes 12582916
  178.0 56.8 %all-to-all-start = ((f32[32,32,1024]{2,1,0:T(8,128)}), f32[32,32,1024]{2,1,0:T(8,128)}, u32[]{:S(2)}, u32[]{:S(2)}) async-start(f32[32,32,1024]{2,1,0:T(8,128)} %stack.2), calls=%async_computation | async-start | bytes 8388608 | tf_op jit(solution)/shard_map/all_to_all | solution.py:44
Sparse Core Ops, SparseCore 0:
  14.7 125.5 all-reduce.1

commit v2 on v0

--- a/solution.py
+++ b/solution.py
@@ -26,7 +26,7 @@
     placed = lax.dynamic_update_slice_in_dim(
         jnp.zeros((order_size, order_size), jnp.float32), stat_decay * stat_old, offset, 0
     )
-    stat_whole = lax.psum(weight_new * partial_value + placed, ("col", "pan"))
+    stat_whole = lax.psum(lax.psum(weight_new * partial_value + placed, "pan"), "col")
     stat_new = lax.dynamic_slice_in_dim(stat_whole, offset, panel_rows, 0)
     matrix = stat_whole + damping * eye_whole
     frobenius = jnp.sqrt(jnp.sum(matrix * matrix))

time: 281 us -> 440 us (1.57)
  waiting for transfers between devices: 212 us -> 371 us
    psum x1 -> x2, waiting for transfers between devices: 126 us -> 282 us  [the longest x1 159 us: local(): lax.psum(lax.psum(weight_new * partial_value + placed, 'pan'), 'col')]
  transfers between devices with their start and end apart: 2 -> 3, of which waited for: 2 -> 3; matrix products, arithmetic and copies ran while one was open for 1% -> 0% of each run, Pallas kernels for 0% -> 0%
where the time goes in v2:
time: 440 us; the launch traced here: 439 us
  waiting for transfers between devices  371 us (84%)
  matrix products  45.2 us (10%)
  between operations  14.6 us (3%)
  other arithmetic  5.45 us (1%)
    psum x1, waiting for transfers between devices, local(): lax.psum(lax.psum(weight_new * partial_value + placed, 'pan'), 'col')  159 us
    psum x1, waiting for transfers between devices, local(): lax.psum(weight_new * partial_value + placed, 'pan')  123 us
    all_gather x1, waiting for transfers between devices, local(): lax.all_gather(root_panel, ('col', 'pan'), axis=0, tiled=True)  88.6 us
    dot_general x1, matrix products, local(): square = jnp.dot(first_step, first_step, precision=highest)  19.9 us
    dot_general x1, matrix products, local(): jnp.dot(lax.all_gather(root_panel, ('col', 'pan'), axis=0, tiled=True), g...  9.65 us
  transfers between devices with their start and end apart: 3, of which 3 were waited for; matrix products, arithmetic and copies ran while one was open for 0% of the time, Pallas kernels for 0%

profile of v2, /device:TPU:1, one launch (start us, length us, event | category | flops | bytes accessed | tf_op | source)
XLA Modules:
  0.0 439.4 jit_solution(8817099831153086468)
XLA Ops:
  7.2 0.0 copy-start
  7.2 0.0 all-reduce.3.cloned.1.call-start
  7.2 1.4 copy-done
  8.7 0.0 copy-start.2
  8.7 4.3 convolution_multiply_fusion
  13.0 0.0 copy-done.2
  13.0 1.6 add_dynamic-update-slice_fusion
  14.6 0.0 all-reduce.3.cloned.1.call-update
  14.6 0.0 all-reduce.5.cloned.1.call-start
  14.7 123.4 %all-reduce.3.cloned.1.call-done = f32[1024,1024]{1,0:T(8,128)} async-done(((f32[1024,1024]{1,0:T(8,128)}), f32[1024,1024]{1,0:T(8,128)}) %all-reduce.3.cloned.1.call-update) | async-done | bytes 4194320 | tf_op jit(solution)/shard_map/psum | solution.py:29
  138.0 0.0 all-reduce.5.cloned.1.call-update
  138.0 0.0 all-gather.2.cloned.1.call-start
  138.1 159.0 %all-reduce.5.cloned.1.call-done = f32[1024,1024]{1,0:T(8,128)} async-done(((f32[1024,1024]{1,0:T(8,128)}), f32[1024,1024]{1,0:T(8,128)}) %all-reduce.5.cloned.1.call-update) | async-done | bytes 4194320 | tf_op jit(solution)/shard_map/psum | solution.py:29
  297.1 3.9 multiply_reduce_fusion
  301.7 19.9 %fusion.1 = f32[1024,1024]{1,0:T(8,128)S(1)} fusion(f32[1024,1024]{1,0:T(8,128)} %all-reduce.5.cloned.1.call-done, f32[]{:T(128)S(6)} %sqrt.3), kind=kOutput, calls=%fused_computation.6 | convolution fusion | flops 12893290496 | bytes 8388612 | tf_op jit(solution)/shard_map/dot_general | solution.py:35
  321.6 2.5 fusion.10
  324.1 0.0 copy-start.1
  324.1 5.1 %fusion.8 = f32[32,1024]{1,0:T(8,128)S(1)} fusion(f32[32,1024]{1,0:T(8,128)S(1)} %fusion.10, s32[32]{0:T(128)S(1)} %iota_add_fusion, f32[1024,1024]{1,0:T(8,128)} %all-reduce.5.cloned.1.call-done, f32[]{:T(128)S(6)} %sqrt.3), kind=kOutput, calls=%fused_computation.15 | convolution fusion | flops 408027136 | bytes 4456580 | tf_op jit(solution)/shard_map/dot_general | solution.py:38
  329.3 0.0 copy-done.1
  329.3 3.7 fusion.9
  333.0 0.0 all-gather.2.cloned.1.call-update
  333.0 1.6 constant_dynamic-slice_fusion
  334.6 88.6 %all-gather.2.cloned.1.call-done = f32[1024,1024]{1,0:T(8,128)} async-done(((f32[32,1024]{1,0:T(8,128)}), f32[1024,1024]{1,0:T(8,128)}) %all-gather.2.cloned.1.call-update) | async-done | bytes 4194320 | tf_op jit(solution)/shard_map/all_gather | solution.py:43
  423.2 9.6 %fusion.19 = f32[1024,896]{1,0:T(8,128)} fusion(f32[1024,1024]{1,0:T(8,128)} %all-gather.2.cloned.1.call-done, bf16[1024,896]{1,0:T(8,128)(2,1)S(1)} %copy-done), kind=kOutput, calls=%fused_computation.30 | convolution fusion | flops 11274289152 | bytes 9699328 | tf_op jit(solution)/shard_map/dot_general | solution.py:42
  (1 shorter events, 0.0 us)
Async XLA Ops:
  7.2 1.5 copy-start
  7.2 130.8 %all-reduce.3.cloned.1.call-start = ((), (), s32[]{:S(2)}) async-start(), calls=%async_computation | async-start | bytes 8388608 | tf_op jit(solution)/shard_map/psum | solution.py:29
  8.7 4.3 copy-start.2
  14.6 282.5 %all-reduce.5.cloned.1.call-start = ((), (), s32[]{:S(2)}) async-start(), calls=%async_computation.1 | async-start | bytes 8388608 | tf_op jit(solution)/shard_map/psum | solution.py:29
  138.0 285.1 %all-gather.2.cloned.1.call-start = ((), (), s32[]{:S(2)}) async-start(), calls=%async_computation.2 | async-start | bytes 4325376 | tf_op jit(solution)/shard_map/all_gather | solution.py:43
  324.1 5.1 %copy-start.1 = (f32[1024,1024]{1,0:T(8,128)S(1)}, f32[1024,1024]{1,0:T(8,128)}, u32[]{:S(2)}) copy-start(f32[1024,1024]{1,0:T(8,128)} %all-reduce.5.cloned.1.call-done) | copy-start | bytes 12582916
Sparse Core Ops, SparseCore 0:
  14.7 123.2 all-reduce.2
  140.7 156.3 all-reduce.4
  333.2 89.9 all-gather.1
